TPU v7x, 256 devices: a whole 4x4x8 slice. The times are simulated.
256 devices in a mesh: src: 128 (over x, z, y), lev: 2 (over core).
Axes of the slice: x: 4, y: 4, z: 8, core: 2. Of those that a mesh axis runs over, the one named last changes fastest.
Arguments:
- field: bfloat16 [262144, 256], P('src', 'lev'), may hold values from -6 to 6
- grad_coef: float32 [2, 4, 262144], P(None, None, 'src'), may hold values from -6 to 6
- neighbours: int32 [262144, 4], P('src'), may hold values from 0 to 2175, as said below
- level_weight: float32 [8], replicated, may hold values from 0.2 to 2
- src_index: int32 [16384, 64], P('src'), may hold values from 0 to 2047
- tgt_index: int32 [16384, 32], P('src'), may hold values from 0 to 1023
- block_dest: int32 [16384, 1], P('src'), may hold values from 0 to 127; in each aligned block of 128 rows (0 to 127, 128 to 255, ...) at most 2 rows name the same one
- weights: bfloat16 [16384, 6144], P('src'), may hold values from -0.21875 to 0.21875
Outputs:
- remapped: bfloat16 [131072, 256], P('src', 'lev')
- column_total: float32 [32, 131072], P(None, 'src')
Inputs may be any that keep to these rules, and one draw needn't show every extreme that they name: `neighbours`: position 64 + p is the device's own cell p; positions below 64 and from 2112 on are the last and first cells of the devices before and after along the closed curve; a neighbour lies at most 64 cells from the cell. `block_dest`: the 128 blocks of one index of src name one target index at most 2 times.
All inputs are finite; a program needn't handle non-finite values.
Results may differ from a plain program's by a relative error of at most 0.0049.
Values may be sent and summed in bfloat16 or wider, within the bound.
No kernel may reach another device: no remote copies, remote signals or barrier semaphores. Data moves between devices by JAX's collectives and lax.ppermute only.
A program may use at most 128 MiB of HBM per device.

v0:
```python
import jax
import jax.numpy as jnp
from jax import lax
from jax.sharding import PartitionSpec as P

FIELDS = 32
HW = 64
SB = 64
TB = 32
T_DEV = 1024


def extended_2(block, sides, width):
    for axis, dim in sides:
        count = lax.axis_size(axis)
        forward = [(i, i + 1) for i in range(count - 1)]
        forward.append((count - 1, 0))
        backward = [(target, source) for source, target in forward]
        low = lax.ppermute(
            lax.slice_in_dim(block, block.shape[dim] - width, None, axis=dim), axis, forward
        )
        high = lax.ppermute(lax.slice_in_dim(block, 0, width, axis=dim), axis, backward)
        block = jnp.concatenate([low, block, high], axis=dim)
    return block


def block_product(block_weights, block_rows):
    block_count = block_rows.shape[0]
    shaped = block_weights.reshape(block_count, 3 * SB, TB)
    return lax.dot_general(
        shaped, block_rows, (((1,), (1,)), ((0,), (0,))), preferred_element_type=jnp.float32
    )


def shards(field, grad_coef, neighbours, level_weight, src_index, tgt_index, block_dest, weights):
    extended = extended_2(field, (("src", 0),), HW)
    own_float = field.astype(jnp.float32)
    differ = extended[neighbours].astype(jnp.float32) - own_float[:, None, :]
    grad_east = jnp.sum(grad_coef[0].T[:, :, None] * differ, axis=1).astype(jnp.bfloat16)
    grad_north = jnp.sum(grad_coef[1].T[:, :, None] * differ, axis=1).astype(jnp.bfloat16)
    recon = jnp.stack([field, grad_east, grad_north])
    columns = field.shape[1]
    block_count = src_index.shape[0]
    block_rows = jnp.transpose(recon[:, src_index], (1, 0, 2, 3)).reshape(
        block_count, 3 * SB, columns
    )
    src_count = lax.axis_size("src")
    capacity = 2 * block_count // src_count
    target_owner = block_dest[:, 0]
    onehot = (target_owner[:, None] == jnp.arange(src_count, dtype=jnp.int32)[None, :]).astype(
        jnp.int32
    )
    before = jnp.cumsum(onehot, axis=0) - onehot
    slot_rank = jnp.sum(before * onehot, axis=1)
    slot_index = target_owner * capacity + slot_rank
    slots = src_count * capacity
    send_cells = jnp.zeros((slots, TB), jnp.int32).at[slot_index].set(tgt_index)
    recv_cells = lax.all_to_all(send_cells, "src", split_axis=0, concat_axis=0, tiled=True)
    send_rows = jnp.zeros((slots, 3 * SB, columns), jnp.bfloat16).at[slot_index].set(block_rows)
    send_weights = jnp.zeros((slots, weights.shape[1]), jnp.bfloat16).at[slot_index].set(weights)
    got_rows, got_weights = (
        lax.all_to_all(send_rows, "src", split_axis=0, concat_axis=0, tiled=True),
        lax.all_to_all(send_weights, "src", split_axis=0, concat_axis=0, tiled=True),
    )
    received = block_product(got_weights, got_rows)
    total = (
        jnp.zeros((T_DEV, columns), jnp.float32)
        .at[recv_cells.reshape(-1)]
        .add(received.reshape(-1, columns))
    )
    remapped = total.astype(jnp.bfloat16)
    level_count = columns // FIELDS
    level_share = lax.dynamic_slice_in_dim(
        level_weight, lax.axis_index("lev") * level_count, level_count
    )
    local_sum = jnp.einsum(
        "tlf,l->ft",
        total.reshape(T_DEV, level_count, FIELDS),
        level_share,
        precision=lax.Precision.HIGHEST,
    )
    column_total = lax.psum(local_sum, "lev")
    return (remapped, column_total)


def solution(mesh):
    placed = (
        P("src", "lev"),
        P(None, None, "src"),
        P("src", None),
        P(),
        P("src", None),
        P("src", None),
        P("src", None),
        P("src", None),
    )
    return jax.shard_map(
        shards,
        mesh=mesh,
        in_specs=placed,
        out_specs=(P("src", "lev"), P(None, "src")),
        check_vma=False,
    )
```

profile of v0, /device:TPU:1, one launch (start us, length us, event | category | flops | bytes accessed | tf_op | source)
XLA Modules:
  0.0 694.2 jit_solution(10365732698928579888)
XLA Ops:
  8.1 0.8 select_reduce_fusion
  9.6 0.8 copy.21
  10.4 1.5 scatter_custom_fusion
  11.9 16.3 %all-to-all-start = ((s32[128,2,32]{2,1,0:T(2,128)}), s32[128,2,32]{2,1,0:T(2,128)S(1)}, u32[]{:S(2)}, u32[]{:S(2)}) async-start(s32[128,2,32]{2,1,0:T(2,128)} %bitcast.3), calls=%async_computation | async-start | bytes 262144 | tf_op jit(solution)/shard_map/all_to_all | solution.py:58
  28.2 4.6 scatter_custom_fusion.1
  32.9 3.3 all_to_all.17
  36.2 3.0 all-to-all-done
  39.2 10.9 %all-to-all-start.1 = ((bf16[128,2,6144]{2,1,0:T(2,128)(2,1)}), bf16[128,2,6144]{2,1,0:T(2,128)(2,1)}, u32[]{:S(2)}, u32[]{:S(2)}) async-start(bf16[128,2,6144]{2,1,0:T(2,128)(2,1)} %all_to_all.17), calls=%async_computation.1 | async-start | bytes 6291456 | tf_op jit(solution)/shard_map/all_to_all | solution.py:63
  50.7 6.5 collective-permute-start.1
  58.5 1.1 convert_element_type.40
  59.6 1.4 copy.22
  61.0 1.4 copy.24
  62.3 8.9 %copy.25 = bf16[1,2048,128]{2,0,1:T(2,128)(2,1)} copy(bf16[1,2048,128]{2,1,0:T(8,128)(2,1)S(1)} %bitcast.44) | data formatting | bytes 1048576 | tf_op jit(solution)/shard_map/stack | solution.py:41
  71.2 49.7 %collective-permute-done = bf16[64,128]{1,0:T(8,128)(2,1)S(1)} collective-permute-done((bf16[64,128]{1,0:T(8,128)(2,1)S(1)}, bf16[64,128]{1,0:T(8,128)(2,1)S(1)}, u32[]{:S(2)}, u32[]{:S(2)}) %collective-permute-start) | collective-permute-done | bytes 16416 | tf_op jit(solution)/shard_map/ppermute | solution.py:19
  121.0 24.0 %gather_fusion = bf16[8192,128]{1,0:T(8,128)(2,1)S(1)} fusion(bf16[2176,128]{1,0:T(8,128)(2,1)S(1)} %pad_maximum_fusion.1, s32[8192]{0:T(1024)S(1)} %broadcast_clamp_fusion.1), kind=kCustom, calls=%fused_computation | custom fusion | bytes 4227072 | tf_op jit(solution)/shard_map/gather | solution.py:38
  145.1 15.1 %fusion.2 = (bf16[2048,128]{1,0:T(8,128)(2,1)S(1)}, bf16[2048,128]{1,0:T(8,128)(2,1)S(1)}) fusion(bf16[2048,4,128]{2,1,0:T(4,128)(2,1)S(1)} %bitcast.43, f32[2048,128]{1,0:T(8,128)} %convert_element_type.40, f32[2048,4]{1,0:T(8,128)} %copy.22, f32[2048,4]{1,0:T(8,128)} %copy.24), kind=kLoop, calls=%fused_computation.9 | loop fusion | flops 5767168 | bytes 4259840 | tf_op jit(solution)/shard_map/reduce_sum | solution.py:39
  160.1 8.1 %copy.26 = bf16[1,2048,128]{2,0,1:T(2,128)(2,1)S(1)} copy(bf16[1,2048,128]{2,1,0:T(8,128)(2,1)S(1)} %bitcast.47) | data formatting | bytes 1048576 | tf_op jit(solution)/shard_map/convert_element_type | solution.py:39
  168.3 8.3 %copy.27 = bf16[1,2048,128]{2,0,1:T(2,128)(2,1)S(1)} copy(bf16[1,2048,128]{2,1,0:T(8,128)(2,1)S(1)} %bitcast.46) | data formatting | bytes 1048576 | tf_op jit(solution)/shard_map/convert_element_type | solution.py:40
  176.6 3.6 pad_maximum_fusion
  180.2 56.5 %gather_fusion.1 = bf16[8192,3,128]{2,1,0:T(4,128)(2,1)} fusion(bf16[3,2048,128]{2,0,1:T(4,128)(2,1)S(1)} %pad_maximum_fusion, s32[8192]{0:T(1024)S(1)} %broadcast_clamp_fusion), kind=kCustom, calls=%fused_computation.1 | custom fusion | bytes 12615680 | tf_op jit(solution)/shard_map/gather | solution.py:44
  236.7 8.0 %copy.29 = bf16[128,64,3,128]{3,1,2,0:T(8,128)(2,1)} copy(bf16[128,64,3,128]{3,2,1,0:T(4,128)(2,1)} %bitcast.40) | data formatting | bytes 12582912 | tf_op jit(solution)/shard_map/gather | solution.py:44
  244.7 7.8 %broadcast_in_dim.29 = bf16[256,192,128]{2,1,0:T(8,128)(2,1)} broadcast(bf16[]{:T(256)} %constant.16.clone.1), dimensions={} | broadcast | bytes 12582914 | tf_op jit(solution)/shard_map/broadcast_in_dim | solution.py:59
  252.5 21.5 %scatter_fusion = bf16[256,192,128]{2,1,0:T(8,128)(2,1)} fusion(bf16[256,192,128]{2,1,0:T(8,128)(2,1)} %broadcast_in_dim.29, s32[128]{0:T(128)S(1)} %fusion.13, bf16[128,192,128]{2,1,0:T(8,128)(2,1)} %bitcast.41), kind=kCustom, calls=%fused_computation.4 | custom fusion | bytes 18874880 | tf_op jit(solution)/shard_map/scatter | solution.py:59
  274.0 9.3 %all-to-all-start.2 = ((bf16[256,192,128]{2,1,0:T(8,128)(2,1)}), bf16[256,192,128]{2,1,0:T(8,128)(2,1)}, u32[]{:S(2)}, u32[]{:S(2)}) async-start(bf16[256,192,128]{2,1,0:T(8,128)(2,1)} %scatter_fusion), calls=%async_computation.2 | async-start | bytes 25165824 | tf_op jit(solution)/shard_map/all_to_all | solution.py:62
  283.6 16.2 %reshape.74 = bf16[256,192,32]{2,1,0:T(8,128)(2,1)} reshape(bf16[128,2,6144]{2,1,0:T(2,128)(2,1)} %all-to-all-done.1) | data formatting | bytes 6291456 | tf_op jit(solution)/shard_map/reshape | solution.py:29
  299.8 256.5 %all-to-all-done.2 = bf16[256,192,128]{2,1,0:T(8,128)(2,1)} async-done(((bf16[256,192,128]{2,1,0:T(8,128)(2,1)}), bf16[256,192,128]{2,1,0:T(8,128)(2,1)}, u32[]{:S(2)}, u32[]{:S(2)}) %all-to-all-start.2) | async-done | bytes 12582944 | tf_op jit(solution)/shard_map/all_to_all | solution.py:62
  556.3 12.1 %fusion.17 = f32[256,32,128]{2,1,0:T(8,128)} fusion(bf16[256,192,32]{2,1,0:T(8,128)(2,1)} %reshape.74, bf16[256,192,128]{2,1,0:T(8,128)(2,1)} %all-to-all-done.2), kind=kOutput, calls=%fused_computation.39 | convolution fusion | flops 402653184 | bytes 19922944 | tf_op jit(solution)/shard_map/dot_general | solution.py:30
  568.4 49.1 %scatter_custom_fusion.3 = f32[1024,128]{1,0:T(8,128)S(1)} fusion(s32[8192]{0:T(1024)S(1)} %bitcast.49, f32[8192,128]{1,0:T(8,128)} %bitcast.42, f32[]{:T(128)} %constant.11.clone.1), kind=kCustom, calls=%fused_computation.19 | custom fusion | flops 1048576 | bytes 524800 | tf_op jit(solution)/shard_map/scatter-add | solution.py:69
  617.7 28.9 %fusion.6 = f32[1,1024,32]{0,1,2:T(8,128)} fusion(f32[1024,4,32]{0,2,1:T(8,128)S(1)} %bitcast.45, f32[8]{0:T(128)S(1)} %copy-done, s32[]{:T(128)S(6)} %select_n.29), kind=kOutput, calls=%fused_computation.15 | convolution fusion | flops 1572864 | bytes 655396 | tf_op jit(solution)/shard_map/tlf,l->ft/dot_general | solution.py:76
  646.6 10.6 %copy.34 = f32[1,1024,32]{1,2,0:T(8,128)} copy(f32[1,1024,32]{0,1,2:T(8,128)} %fusion.6) | data formatting | bytes 262144 | tf_op jit(solution)/shard_map/tlf,l->ft/dot_general | solution.py:76
  658.0 27.4 %all-reduce.2.cloned.1.call-done = f32[32,1024]{1,0:T(8,128)} async-done(((f32[32,1024]{1,0:T(8,128)}), f32[32,1024]{1,0:T(8,128)}) %all-reduce.2.cloned.1.call-update) | async-done | bytes 131088 | tf_op jit(solution)/shard_map/psum | solution.py:82
  685.3 1.6 copy.39
  (35 shorter events, 4.6 us)
Async XLA Ops:
  7.2 610.6 %copy-start = (f32[8]{0:T(128)S(1)}, f32[8]{0:T(128)}, u32[]{:S(2)}) copy-start(f32[8]{0:T(128)} %param.11) | copy-start | bytes 100
  11.9 27.3 %all-to-all-start = ((s32[128,2,32]{2,1,0:T(2,128)}), s32[128,2,32]{2,1,0:T(2,128)S(1)}, u32[]{:S(2)}, u32[]{:S(2)}) async-start(s32[128,2,32]{2,1,0:T(2,128)} %bitcast.3), calls=%async_computation | async-start | bytes 262144 | tf_op jit(solution)/shard_map/all_to_all | solution.py:58
  36.2 13.9 %copy-start.1 = (bf16[2048,128]{1,0:T(8,128)(2,1)S(1)}, bf16[2048,128]{1,0:T(8,128)(2,1)}, u32[]{:S(2)}) copy-start(bf16[2048,128]{1,0:T(8,128)(2,1)} %param.8) | copy-start | bytes 1572868
  36.2 21.0 %copy-start.4 = (s32[2048,4]{0,1:T(4,128)S(1)}, s32[2048,4]{0,1:T(4,128)}, u32[]{:S(2)}) copy-start(s32[2048,4]{0,1:T(4,128)} %param.10) | copy-start | bytes 98308
  36.2 22.1 %copy-start.5 = (s32[128,64]{0,1:T(8,128)S(1)}, s32[128,64]{0,1:T(8,128)}, u32[]{:S(2)}) copy-start(s32[128,64]{0,1:T(8,128)} %param.12) | copy-start | bytes 98308
  36.2 22.3 %copy-start.3 = (f32[2,4,2048]{2,1,0:T(4,128)S(1)}, f32[2,4,2048]{2,1,0:T(4,128)}, u32[]{:S(2)}) copy-start(f32[2,4,2048]{2,1,0:T(4,128)} %param.9) | copy-start | bytes 196612
  39.2 234.8 %all-to-all-start.1 = ((bf16[128,2,6144]{2,1,0:T(2,128)(2,1)}), bf16[128,2,6144]{2,1,0:T(2,128)(2,1)}, u32[]{:S(2)}, u32[]{:S(2)}) async-start(bf16[128,2,6144]{2,1,0:T(2,128)(2,1)} %all_to_all.17), calls=%async_computation.1 | async-start | bytes 6291456 | tf_op jit(solution)/shard_map/all_to_all | solution.py:63
  50.1 70.9 %collective-permute-start = (bf16[64,128]{1,0:T(8,128)(2,1)S(1)}, bf16[64,128]{1,0:T(8,128)(2,1)S(1)}, u32[]{:S(2)}, u32[]{:S(2)}) collective-permute-start(bf16[64,128]{1,0:T(8,128)(2,1)S(1)} %get-tuple-element.4), channel_id=1, source_target_pairs={{0,2},{2,4},{4,6},{6,8},{8,10},{10,12},{12,14},{14,16},{16,18},{18... | collective-permute-start | bytes 49160 | tf_op jit(solution)/shard_map/ppermute | solution.py:19
  50.7 70.3 %collective-permute-start.1 = (bf16[64,128]{1,0:T(8,128)(2,1)S(1)}, bf16[64,128]{1,0:T(8,128)(2,1)S(1)}, u32[]{:S(2)}, u32[]{:S(2)}) collective-permute-start(bf16[64,128]{1,0:T(8,128)(2,1)S(1)} %get-tuple-element.5), channel_id=1, source_target_pairs={{2,0},{4,2},{6,4},{8,6},{10,8},{12,10},{14,12},{16,14},{18,16},{20... | collective-permute-start | bytes 49160 | tf_op jit(solution)/shard_map/ppermute | solution.py:22
  145.1 31.6 %copy-start.2 = (bf16[1,2048,128]{2,0,1:T(2,128)(2,1)S(1)}, bf16[1,2048,128]{2,0,1:T(2,128)(2,1)}, u32[]{:S(2)}) copy-start(bf16[1,2048,128]{2,0,1:T(2,128)(2,1)} %copy.25) | copy-start | bytes 1572868
  274.0 282.3 %all-to-all-start.2 = ((bf16[256,192,128]{2,1,0:T(8,128)(2,1)}), bf16[256,192,128]{2,1,0:T(8,128)(2,1)}, u32[]{:S(2)}, u32[]{:S(2)}) async-start(bf16[256,192,128]{2,1,0:T(8,128)(2,1)} %scatter_fusion), calls=%async_computation.2 | async-start | bytes 25165824 | tf_op jit(solution)/shard_map/all_to_all | solution.py:62
  283.3 402.0 %all-reduce.2.cloned.1.call-start = ((), (), s32[]{:S(2)}) async-start(), calls=%async_computation.3 | async-start | bytes 262144 | tf_op jit(solution)/shard_map/psum | solution.py:82
Sparse Core Ops, SparseCore 0:
  657.3 27.9 all-reduce.1
where the time goes:
time: 703 us; the launch traced here: 694 us
  waiting for transfers between devices  337 us (48%)
  local copies, waits for them, and re-layouts  186 us (26%)
  other arithmetic  72.1 us (10%)
  starting transfers between devices  43.7 us (6%)
  matrix products  40.9 us (6%)
  between operations  14.7 us (2%)
    all_to_all x1, waiting for transfers between devices, shards(): lax.all_to_all(send_rows, 'src', split_axis=0, concat_axis=0, tiled=True)  257 us
    gather x2, local copies, waits for them, and re-layouts, shards(): recon[:, src_index]  64.5 us
    ppermute x1, waiting for transfers between devices, extended_2(): lax.ppermute(lax.slice_in_dim(block, block.shape[dim] - width, None, axis...  49.7 us
    scatter-add x1, other arithmetic, shards(): total = jnp.zeros((T_DEV, columns), jnp.float32).at[recv_cells.reshape(-1...  49.1 us
    dot_general x1, matrix products, shards(): jnp.einsum('tlf,l->ft', total.reshape(T_DEV, level_count, FIELDS), level_...  28.9 us
    psum x1, waiting for transfers between devices, shards(): column_total = lax.psum(local_sum, 'lev')  27.4 us
    gather x1, local copies, waits for them, and re-layouts, shards(): differ = extended[neighbours].astype(jnp.float32) - own_float[:, None, :]  24 us
    scatter x1, local copies, waits for them, and re-layouts, shards(): jnp.zeros((slots, 3 * SB, columns), jnp.bfloat16).at[slot_index]  21.5 us
  transfers between devices with their start and end apart: 6, of which 4 were waited for; matrix products, arithmetic and copies ran while one was open for 27% of the time, Pallas kernels for 0%

commit v1 on v0

v1 whole, which is shorter than its diff:
```python
import jax
import jax.numpy as jnp
from jax import lax
from jax.experimental import pallas as pl
from jax.experimental.pallas import tpu as pltpu
from jax.sharding import PartitionSpec as P

FIELDS = 32
HW = 64
SB = 64
TB = 32
K = 4
S_DEV = 2048
T_DEV = 1024
B_DEV = 128
N_SRC = 128
COLS = 128
CAP = 2
TILE = 128
PITCH = 49
ROWS = 72
GROUP = 8
F32 = jnp.float32
BF16 = jnp.bfloat16

TN = (((0,), (0,)), ((), ()))
NN = (((1,), (0,)), ((), ()))
NT = (((1,), (1,)), ((), ()))


def source_kernel(
    src_ref,
    dest_ref,
    parity_ref,
    field_ref,
    low_ref,
    high_ref,
    coef_ref,
    nbr_ref,
    tgt_ref,
    w_ref,
    out_ref,
    ext,
    tab,
    wrows,
    xa,
    xb,
    cells,
    count,
):
    ext[0:HW, :] = low_ref[...]
    ext[HW : HW + S_DEV, :] = field_ref[...]
    ext[HW + S_DEV :, :] = high_ref[...]

    def spread(g, _):
        rows = w_ref[pl.ds(pl.multiple_of(g * 8, 8), 8), :].astype(F32)
        for q in range(48):
            wrows[pl.ds(g * (8 * PITCH) + q, 8, stride=PITCH), :] = rows[:, q * 128 : (q + 1) * 128]
        return 0

    lax.fori_loop(0, B_DEV // 8, spread, 0)

    position = lax.broadcasted_iota(jnp.int32, (2 * TILE, TILE), 0)
    lane = lax.broadcasted_iota(jnp.int32, (2 * TILE, TILE), 1)

    def gradients(t, _):
        p0 = pl.multiple_of(t * TILE, TILE)
        own = position == lane + HW
        near = nbr_ref[:, pl.ds(p0, TILE)] - p0
        east = jnp.zeros((2 * TILE, TILE), F32)
        north = jnp.zeros((2 * TILE, TILE), F32)
        for k in range(K):
            here = position == near[k : k + 1, :]
            east = east + jnp.where(here, coef_ref[0, k : k + 1, pl.ds(p0, TILE)], 0.0)
            north = north + jnp.where(here, coef_ref[1, k : k + 1, pl.ds(p0, TILE)], 0.0)
        sums = jnp.sum(coef_ref[:, :, pl.ds(p0, TILE)], axis=1)
        east = east - jnp.where(own, sums[0:1, :], 0.0)
        north = north - jnp.where(own, sums[1:2, :], 0.0)
        window = ext[pl.ds(p0, 2 * TILE), :]
        tab[pl.ds(p0 * 3, TILE, stride=3), :] = field_ref[pl.ds(p0, TILE), :].astype(F32)
        for c, full in ((1, east), (2, north)):
            top = full.astype(BF16)
            rest = (full - top.astype(F32)).astype(BF16)
            value = lax.dot_general(top, window, TN, preferred_element_type=F32)
            value = value + lax.dot_general(rest, window, TN, preferred_element_type=F32)
            tab[pl.ds(p0 * 3 + c, TILE, stride=3), :] = value.astype(BF16).astype(F32)
        return 0

    lax.fori_loop(0, S_DEV // TILE, gradients, 0)

    def clear(d, _):
        out_ref[d] = jnp.zeros((ROWS, COLS), BF16)
        cells[d] = jnp.zeros((8, 128), F32)
        count[d] = 0
        return 0

    lax.fori_loop(0, N_SRC, clear, 0)

    lanes = lax.broadcasted_iota(jnp.int32, (8, 128), 1) // TB
    sub = lax.broadcasted_iota(jnp.int32, (8, 128), 0)
    quarter = lax.broadcasted_iota(jnp.int32, (48, 128), 1) // TB
    parity = parity_ref[0]

    def gather(b, x):
        for j in range(SB):
            cell = src_ref[j, b]
            x[pl.ds((j % 4) * 48 + j // 4, 3, stride=16), :] = tab[pl.ds(cell * 3, 3), :]

    def product(b, x):
        chunk = wrows[pl.ds(b * PITCH, 48), :]
        spread_w = jnp.concatenate(
            [jnp.where(quarter == a, chunk, 0.0) for a in range(4)], axis=0
        ).astype(BF16)
        wide = lax.dot_general(spread_w, x[...].astype(BF16), TN, preferred_element_type=F32)
        part = wide[0:32] + wide[32:64] + wide[64:96] + wide[96:128]
        d = dest_ref[b, 0]
        rank = count[d]
        count[d] = rank + 1
        out_ref[d, pl.ds(pl.multiple_of(rank * TB, TB), TB), :] = part.astype(BF16)
        target = jnp.broadcast_to(tgt_ref[pl.ds(b, 1), :], (8, 128))
        pieces = jnp.where(sub == 0, target // 32, target % 32).astype(F32)
        mine = (lanes == parity * 2 + rank) & (sub < 2)
        cells[d] = jnp.where(mine, pieces, cells[d])

    gather(0, xa)

    def pair(i, _):
        b = i * 2
        gather(b + 1, xb)
        product(b, xa)
        gather(jnp.minimum(b + 2, B_DEV - 1), xa)
        product(b + 1, xb)
        return 0

    lax.fori_loop(0, B_DEV // 2, pair, 0)

    def finish(d, _):
        out_ref[d, CAP * TB : ROWS, :] = cells[d].astype(BF16)
        return 0

    lax.fori_loop(0, N_SRC, finish, 0)


def source_side(field, low, high, grad_coef, neighbours, src_index, tgt_index, block_dest, weights, parity):
    vmem = pl.BlockSpec(memory_space=pltpu.VMEM)
    smem = pl.BlockSpec(memory_space=pltpu.SMEM)
    return pl.pallas_call(
        source_kernel,
        out_shape=jax.ShapeDtypeStruct((N_SRC, ROWS, COLS), BF16),
        in_specs=[smem, smem, smem] + [vmem] * 7,
        out_specs=vmem,
        scratch_shapes=[
            pltpu.VMEM((S_DEV + 2 * HW, COLS), BF16),
            pltpu.VMEM((S_DEV * 3 + 8, COLS), F32),
            pltpu.VMEM((B_DEV * PITCH, 128), F32),
            pltpu.VMEM((3 * SB, COLS), F32),
            pltpu.VMEM((3 * SB, COLS), F32),
            pltpu.VMEM((N_SRC, 8, 128), F32),
            pltpu.SMEM((N_SRC,), jnp.int32),
        ],
        compiler_params=pltpu.CompilerParams(vmem_limit_bytes=48 << 20),
        name="source_side",
    )(
        src_index.T,
        block_dest,
        parity,
        field,
        low,
        high,
        grad_coef,
        neighbours.T,
        jnp.tile(tgt_index, (1, 4)),
        weights,
    )


def target_kernel(recv_ref, level_ref, out_ref, column_ref, acc):
    acc[...] = jnp.zeros_like(acc)
    low = lax.broadcasted_iota(jnp.int32, (32, 128), 0).astype(F32)

    def step(g, _):
        base = g * GROUP
        hot = []
        data = []
        for m in range(GROUP // 2):
            first, second = recv_ref[base + 2 * m], recv_ref[base + 2 * m + 1]
            data += [first[0 : CAP * TB], second[0 : CAP * TB]]
            cell = first[CAP * TB :].astype(F32) + second[CAP * TB :].astype(F32)
            top, bottom = cell[0:1, :], cell[1:2, :]
            inner = jnp.where(low == bottom, 1.0, 0.0).astype(BF16)
            hot.append(
                jnp.concatenate(
                    [jnp.where(jnp.broadcast_to(top, (32, 128)) == float(h), 1.0, 0.0).astype(BF16) * inner for h in range(32)],
                    axis=0,
                )
            )
        acc[...] += lax.dot_general(
            jnp.concatenate(hot, axis=1),
            jnp.concatenate(data, axis=0),
            NN,
            preferred_element_type=F32,
        )
        return 0

    lax.fori_loop(0, N_SRC // GROUP, step, 0)
    out_ref[...] = acc[...].astype(BF16)
    column_ref[...] = lax.dot_general(
        level_ref[...], acc[...], NT, preferred_element_type=F32, precision=lax.Precision.HIGHEST
    )


def target_side(recv, level_rows):
    vmem = pl.BlockSpec(memory_space=pltpu.VMEM)
    return pl.pallas_call(
        target_kernel,
        out_shape=(
            jax.ShapeDtypeStruct((T_DEV, COLS), BF16),
            jax.ShapeDtypeStruct((FIELDS, T_DEV), F32),
        ),
        in_specs=[vmem, vmem],
        out_specs=(vmem, vmem),
        scratch_shapes=[pltpu.VMEM((T_DEV, COLS), F32)],
        compiler_params=pltpu.CompilerParams(vmem_limit_bytes=48 << 20),
        name="target_side",
    )(recv, level_rows)


def shards(field, grad_coef, neighbours, level_weight, src_index, tgt_index, block_dest, weights):
    count = lax.axis_size("src")
    forward = [(i, (i + 1) % count) for i in range(count)]
    backward = [(t, s) for s, t in forward]
    low = lax.ppermute(field[S_DEV - HW :], "src", forward)
    high = lax.ppermute(field[:HW], "src", backward)
    parity = (lax.axis_index("src") % 2).reshape(1)
    send = source_side(
        field, low, high, grad_coef, neighbours, src_index, tgt_index, block_dest, weights, parity
    )
    recv = lax.all_to_all(send, "src", split_axis=0, concat_axis=0, tiled=True)
    levels = COLS // FIELDS
    share = lax.dynamic_slice_in_dim(level_weight, lax.axis_index("lev") * levels, levels)
    eye = jnp.eye(FIELDS, dtype=F32)
    level_rows = (eye[:, None, :] * share[None, :, None]).reshape(FIELDS, COLS)
    remapped, local_sum = target_side(recv, level_rows)
    other = lax.ppermute(local_sum, "lev", [(0, 1), (1, 0)])
    return remapped, local_sum + other


def solution(mesh):
    placed = (
        P("src", "lev"),
        P(None, None, "src"),
        P("src", None),
        P(),
        P("src", None),
        P("src", None),
        P("src", None),
        P("src", None),
    )
    return jax.shard_map(
        shards,
        mesh=mesh,
        in_specs=placed,
        out_specs=(P("src", "lev"), P(None, "src")),
        check_vma=False,
    )
```

time: 703 us -> 134 us (0.19); the launches traced: 694 us -> 134 us
  waiting for transfers between devices: 337 us -> 54.6 us
  local copies, waits for them, and re-layouts: 186 us -> 7.46 us
  other arithmetic: 72.1 us -> 0.69 us
  Pallas kernels: 0 us -> 44.2 us
  matrix products: 40.9 us -> 0 us
  starting transfers between devices: 43.7 us -> 25.9 us
  between operations: 14.7 us -> 0.71 us
    all_to_all x3 -> x1, waiting for transfers between devices: 259 us -> 53.7 us  [shards(): recv = lax.all_to_all(send, 'src', split_axis=0, concat_axis=0, tiled=True)]
    gather x3 -> x0, local copies, waits for them, and re-layouts: 88.5 us -> none  [the longest x2 64.5 us: shards(): recon[:, src_index]]
    scatter-add x1 -> x0, other arithmetic: 49.1 us -> none  [shards(): total = jnp.zeros((T_DEV, columns), jnp.float32).at[recv_cells.reshape(-1...]
    ppermute x2 -> x3, waiting for transfers between devices: 49.7 us -> 0.99 us  [the longest x1 0.99 us: shards(): other = lax.ppermute(local_sum, 'lev', [(0, 1), (1, 0)])]
    pallas_call x0 -> x2, Pallas kernels: none -> 44.2 us  [the longest x1 36 us: source_side(): pl.pallas_call(source_kernel, out_shape=jax.ShapeDtypeStruct((N_SRC, ROWS...]
    dot_general x2 -> x0, matrix products: 40.9 us -> none  [the longest x1 28.9 us: shards(): jnp.einsum('tlf,l->ft', total.reshape(T_DEV, level_count, FIELDS), level_...]
    scatter x3 -> x0, local copies, waits for them, and re-layouts: 27.6 us -> none  [the longest x1 21.5 us: shards(): jnp.zeros((slots, 3 * SB, columns), jnp.bfloat16).at[slot_index]]
    psum x1 -> x0, waiting for transfers between devices: 27.4 us -> none  [shards(): column_total = lax.psum(local_sum, 'lev')]
  transfers between devices with their start and end apart: 6 -> 4, of which waited for: 4 -> 2; matrix products, arithmetic and copies ran while one was open for 27% -> 1% of each run, Pallas kernels for 0% -> 0%
where the time goes in v1:
time: 134 us
  waiting for transfers between devices  54.6 us (41%)
  Pallas kernels  44.2 us (33%)
  starting transfers between devices  25.9 us (19%)
  local copies, waits for them, and re-layouts  7.46 us (6%)
    all_to_all x1, waiting for transfers between devices, shards(): recv = lax.all_to_all(send, 'src', split_axis=0, concat_axis=0, tiled=True)  53.7 us
    pallas_call x1, Pallas kernels, source_side(): pl.pallas_call(source_kernel, out_shape=jax.ShapeDtypeStruct((N_SRC, ROWS...  36 us
    all_to_all x1, starting transfers between devices, shards(): recv = lax.all_to_all(send, 'src', split_axis=0, concat_axis=0, tiled=True)  10 us
    ppermute x1, starting transfers between devices, shards(): high = lax.ppermute(field[:HW], 'src', backward)  8.93 us
    pallas_call x1, Pallas kernels, target_side(): pl.pallas_call(target_kernel, out_shape=(jax.ShapeDtypeStruct((T_DEV, COL...  8.23 us
    unnamed x13, local copies, waits for them, and re-layouts  5.57 us
    ppermute x1, starting transfers between devices, shards(): other = lax.ppermute(local_sum, 'lev', [(0, 1), (1, 0)])  4.77 us
  transfers between devices with their start and end apart: 4, of which 2 were waited for; matrix products, arithmetic and copies ran while one was open for 1% of the time, Pallas kernels for 0%

profile of v1, /device:TPU:1, one launch (start us, length us, event | category | flops | bytes accessed | tf_op | source)
XLA Modules:
  0.0 133.6 jit_solution(8367664173702919479)
XLA Ops:
  0.6 0.7 fusion.1
  1.4 2.1 %collective-permute-start = (bf16[64,128]{1,0:T(8,128)(2,1)S(1)}, bf16[64,128]{1,0:T(8,128)(2,1)S(1)}, u32[]{:S(2)}, u32[]{:S(2)}) collective-permute-start(bf16[64,128]{1,0:T(8,128)(2,1)S(1)} %get-tuple-element.7), channel_id=1, source_target_pairs={{0,2},{2,4},{4,6},{6,8},{8,10},{10,12},{12,14},{14,16},{16,18},{18... | collective-permute-start | bytes 49160 | tf_op jit(solution)/shard_map/ppermute | solution.py:232
  3.5 8.9 %collective-permute-start.1 = (bf16[64,128]{1,0:T(8,128)(2,1)S(1)}, bf16[64,128]{1,0:T(8,128)(2,1)S(1)}, u32[]{:S(2)}, u32[]{:S(2)}) collective-permute-start(bf16[64,128]{1,0:T(8,128)(2,1)S(1)} %get-tuple-element.6), channel_id=1, source_target_pairs={{2,0},{4,2},{6,4},{8,6},{10,8},{12,10},{14,12},{16,14},{18,16},{20... | collective-permute-start | bytes 49160 | tf_op jit(solution)/shard_map/ppermute | solution.py:233
  12.4 0.7 tile.4
  13.1 0.1 copy.13.tgt_ref
  13.2 0.8 copy.12.dest_ref
  14.0 0.0 collective-permute-done.low_ref
  14.0 0.0 collective-permute-done.1.high_ref
  14.0 0.0 copy-start
  14.0 1.4 %copy-done = bf16[128,6144]{1,0:T(8,128)(2,1)S(1)} copy-done((bf16[128,6144]{1,0:T(8,128)(2,1)S(1)}, bf16[128,6144]{1,0:T(8,128)(2,1)}, u32[]{:S(2)}) %copy-start) | copy-done | bytes 1572888
  15.4 0.0 copy-start.1
  15.4 1.0 copy-done.1
  16.5 0.0 copy-start.2
  16.5 0.8 copy-done.2
  17.3 0.0 copy-start.3
  17.3 0.8 copy-done.3
  18.1 0.0 copy-start.4
  18.1 0.8 copy-done.4
  18.8 36.0 %source_side.1 = bf16[128,72,128]{2,1,0:T(8,128)(2,1)} custom-call(s32[64,128]{1,0:T(8,128)S(1)} %bitcast.4, s32[128,1]{1,0:T(8,128)S(1)} %copy.12.dest_ref, s32[1]{0:T(128)} %bitcast.1.parity_ref, bf16[2048,128]{1,0:T(8,128)(2,1)S(1)} %copy-done.1, bf16[64,128]{1,0:T(8,128)(2,1)S(1)} %collective-permute-done.low_ref, ...), custom_call_target="tpu_custom_call" | custom-call | tf_op jit(solution)/shard_map/source_side/pallas_call | solution.py:147
  54.8 0.0 copy-start.5
  54.8 10.0 %all-to-all-start = ((bf16[128,72,128]{2,1,0:T(8,128)(2,1)}), bf16[128,72,128]{2,1,0:T(8,128)(2,1)S(1)}, u32[]{:S(2)}, u32[]{:S(2)}) async-start(bf16[128,72,128]{2,1,0:T(8,128)(2,1)} %source_side.1), calls=%async_computation | async-start | bytes 4718592 | tf_op jit(solution)/shard_map/all_to_all | solution.py:238
  64.9 0.0 copy-done.5
  64.9 0.1 dynamic_slice.3
  65.0 0.1 mul.26
  65.0 0.1 mul.27
  65.2 0.1 mul.24
  65.3 53.7 %all-to-all-done.recv_ref = bf16[128,72,128]{2,1,0:T(8,128)(2,1)S(1)} async-done(((bf16[128,72,128]{2,1,0:T(8,128)(2,1)}), bf16[128,72,128]{2,1,0:T(8,128)(2,1)S(1)}, u32[]{:S(2)}, u32[]{:S(2)}) %all-to-all-start) | async-done | bytes 2359328 | tf_op jit(solution)/shard_map/all_to_all | solution.py:238
  118.9 8.2 %target_side.1 = (bf16[1024,128]{1,0:T(8,128)(2,1)}, f32[32,1024]{1,0:T(8,128)S(1)}) custom-call(bf16[128,72,128]{2,1,0:T(8,128)(2,1)S(1)} %all-to-all-done.recv_ref, f32[32,128]{1,0:T(8,128)S(1)} %broadcast_multiply_fusion.level_ref), custom_call_target="tpu_custom_call" | custom-call | tf_op jit(solution)/shard_map/target_side/pallas_call | solution.py:214
  127.2 4.8 %collective-permute-start.2 = (f32[32,1024]{1,0:T(8,128)S(1)}, f32[32,1024]{1,0:T(8,128)S(1)}, u32[]{:S(2)}, u32[]{:S(2)}) collective-permute-start(f32[32,1024]{1,0:T(8,128)S(1)} %get-tuple-element.5), channel_id=1, source_target_pairs={{0,1},{1,0},{2,3},{3,2},{4,5},{5,4},{6,7},{7,6},{8,9},{9,8},{10,11... | collective-permute-start | bytes 393224 | tf_op jit(solution)/shard_map/ppermute | solution.py:244
  131.9 1.0 collective-permute-done.2
  132.9 0.7 add.12
  (3 shorter events, 0.0 us)
Async XLA Ops:
  1.4 12.6 %collective-permute-start = (bf16[64,128]{1,0:T(8,128)(2,1)S(1)}, bf16[64,128]{1,0:T(8,128)(2,1)S(1)}, u32[]{:S(2)}, u32[]{:S(2)}) collective-permute-start(bf16[64,128]{1,0:T(8,128)(2,1)S(1)} %get-tuple-element.7), channel_id=1, source_target_pairs={{0,2},{2,4},{4,6},{6,8},{8,10},{10,12},{12,14},{14,16},{16,18},{18... | collective-permute-start | bytes 49160 | tf_op jit(solution)/shard_map/ppermute | solution.py:232
  3.5 10.5 %collective-permute-start.1 = (bf16[64,128]{1,0:T(8,128)(2,1)S(1)}, bf16[64,128]{1,0:T(8,128)(2,1)S(1)}, u32[]{:S(2)}, u32[]{:S(2)}) collective-permute-start(bf16[64,128]{1,0:T(8,128)(2,1)S(1)} %get-tuple-element.6), channel_id=1, source_target_pairs={{2,0},{4,2},{6,4},{8,6},{10,8},{12,10},{14,12},{16,14},{18,16},{20... | collective-permute-start | bytes 49160 | tf_op jit(solution)/shard_map/ppermute | solution.py:233
  14.0 1.4 %copy-start = (bf16[128,6144]{1,0:T(8,128)(2,1)S(1)}, bf16[128,6144]{1,0:T(8,128)(2,1)}, u32[]{:S(2)}) copy-start(bf16[128,6144]{1,0:T(8,128)(2,1)} %w_ref.1) | copy-start | bytes 4718596
  15.4 1.0 copy-start.1
  16.5 0.8 copy-start.2
  17.3 0.8 copy-start.3
  18.1 0.8 copy-start.4
  54.8 10.1 %copy-start.5 = (f32[8]{0:T(128)S(1)}, f32[8]{0:T(128)}, u32[]{:S(2)}) copy-start(f32[8]{0:T(128)} %param.11) | copy-start | bytes 100
  54.8 64.1 %all-to-all-start = ((bf16[128,72,128]{2,1,0:T(8,128)(2,1)}), bf16[128,72,128]{2,1,0:T(8,128)(2,1)S(1)}, u32[]{:S(2)}, u32[]{:S(2)}) async-start(bf16[128,72,128]{2,1,0:T(8,128)(2,1)} %source_side.1), calls=%async_computation | async-start | bytes 4718592 | tf_op jit(solution)/shard_map/all_to_all | solution.py:238
  127.2 5.8 %collective-permute-start.2 = (f32[32,1024]{1,0:T(8,128)S(1)}, f32[32,1024]{1,0:T(8,128)S(1)}, u32[]{:S(2)}, u32[]{:S(2)}) collective-permute-start(f32[32,1024]{1,0:T(8,128)S(1)} %get-tuple-element.5), channel_id=1, source_target_pairs={{0,1},{1,0},{2,3},{3,2},{4,5},{5,4},{6,7},{7,6},{8,9},{9,8},{10,11... | collective-permute-start | bytes 393224 | tf_op jit(solution)/shard_map/ppermute | solution.py:244
